TPU v7x, 512 devices: a whole 4x8x8 slice. The times are simulated.
512 devices in a mesh: expert: 64 (over z, y), tensor: 8 (over x, core).
Axes of the slice: x: 4, y: 8, z: 8, core: 2. Of those that a mesh axis runs over, the one named last changes fastest.
Arguments:
- tokens: bfloat16 [3072, 4096], P('expert', 'tensor'), may hold values from -6 to 6
- cotangent: bfloat16 [3072, 4096], P('expert', 'tensor'), may hold values from -6 to 6
- expert_ids: int32 [3072, 8], P('expert'), may hold values from 0 to 63, all different within a row; in each aligned block of 48 rows (0 to 47, 48 to 95, ...) at most 8 rows name the same one
- gate_values: float32 [3072, 8], P('expert'), may hold values from 0.05 to 1
- w_gate: bfloat16 [64, 768, 4096], P('expert', 'tensor'), may hold values from -0.09375 to 0.09375
- w_up: bfloat16 [64, 768, 4096], P('expert', 'tensor'), may hold values from -0.09375 to 0.09375
- w_down: bfloat16 [64, 768, 4096], P('expert', 'tensor'), may hold values from -0.21875 to 0.21875
Outputs:
- grad_tokens: bfloat16 [3072, 4096], P('expert', 'tensor')
- grad_gate: bfloat16 [64, 768, 4096], P('expert', 'tensor')
- grad_up: bfloat16 [64, 768, 4096], P('expert', 'tensor')
- grad_down: bfloat16 [64, 768, 4096], P('expert', 'tensor')
Inputs may be any that keep to these rules, and one draw needn't show every extreme that they name: `expert_ids`: each row names 8 different experts. Among the 48 tokens of one index of the expert axis no expert is named more than 8 times, and in every draw some expert is named exactly 8 times there.
All inputs are finite; a program needn't handle non-finite values.
Results may differ from a plain program's by a relative error of at most 0.019.
Values may be sent and summed in bfloat16 or wider, within the bound.
No kernel may reach another device: no remote copies, remote signals or barrier semaphores. Data moves between devices by JAX's collectives and lax.ppermute only.
A program may use at most 64 MiB of HBM per device.

v0:
```python
import jax
import jax.numpy as jnp
from jax import lax
from jax.sharding import PartitionSpec as P

TOP = 8


def expert_backward(rows_x, rows_d, w_gate, w_up, w_down):
    gate_pre = jnp.einsum("secd,ehd->sech", rows_x, w_gate, preferred_element_type=jnp.float32)
    up_pre = jnp.einsum("secd,ehd->sech", rows_x, w_up, preferred_element_type=jnp.float32)
    sigmoid = jax.nn.sigmoid(gate_pre)
    active = gate_pre * sigmoid
    hidden = (active * up_pre).astype(jnp.bfloat16)
    hidden_grad = jnp.einsum("secd,ehd->sech", rows_d, w_down, preferred_element_type=jnp.float32)
    up_grad = (hidden_grad * active).astype(jnp.bfloat16)
    gate_grad = (hidden_grad * up_pre * sigmoid * (1.0 + gate_pre * (1.0 - sigmoid))).astype(
        jnp.bfloat16
    )
    grad_gate = jnp.einsum(
        "sech,secd->ehd", gate_grad, rows_x, preferred_element_type=jnp.float32
    ).astype(jnp.bfloat16)
    grad_up = jnp.einsum(
        "sech,secd->ehd", up_grad, rows_x, preferred_element_type=jnp.float32
    ).astype(jnp.bfloat16)
    grad_down = jnp.einsum(
        "sech,secd->ehd", hidden, rows_d, preferred_element_type=jnp.float32
    ).astype(jnp.bfloat16)
    partial_value = jnp.einsum(
        "sech,ehd->secd", gate_grad, w_gate, preferred_element_type=jnp.float32
    )
    partial_value = partial_value + jnp.einsum(
        "sech,ehd->secd", up_grad, w_up, preferred_element_type=jnp.float32
    )
    return (partial_value, grad_gate, grad_up, grad_down)


def on_device(tokens, cotangent, expert_ids, gate_values, w_gate, w_up, w_down):
    tok_count = expert_ids.shape[0]
    local_count = w_gate.shape[0]
    groups = lax.axis_size("expert")
    experts = local_count * groups
    capacity = 4 * tok_count * TOP // (3 * experts)
    feat_width = tokens.shape[1]
    flat_ids = expert_ids.reshape(-1)
    onehot = (flat_ids[:, None] == jnp.arange(experts, dtype=jnp.int32)[None, :]).astype(jnp.int32)
    before = jnp.cumsum(onehot, axis=0) - onehot
    slot_pos = jnp.sum(before * onehot, axis=1)
    target = flat_ids * capacity + slot_pos
    matches = (target[None, :] == jnp.arange(experts * capacity, dtype=jnp.int32)[:, None]).reshape(
        experts * capacity, tok_count, TOP
    )
    by_token = jnp.any(matches, axis=2)
    occupied = jnp.any(by_token, axis=1)
    token_iota = jnp.arange(tok_count, dtype=jnp.int32)
    owner = jnp.sum(jnp.where(by_token, token_iota[None, :], 0), axis=1)
    slot_weight = jnp.sum(jnp.sum(jnp.where(matches, gate_values[None, :, :], 0.0), axis=2), axis=1)
    full_x, full_d = (
        lax.all_gather(tokens, "tensor", axis=1, tiled=True),
        lax.all_gather(cotangent, "tensor", axis=1, tiled=True),
    )
    sent_x = jnp.where(occupied[:, None], full_x[owner], jnp.zeros((), jnp.bfloat16))
    sent_d = (slot_weight[:, None] * full_d[owner].astype(jnp.float32)).astype(jnp.bfloat16)
    buffer_shape = (groups, local_count, capacity, full_x.shape[1])
    sent_x, sent_d = (sent_x.reshape(buffer_shape), sent_d.reshape(buffer_shape))
    rows_x, rows_d = (
        lax.all_to_all(sent_x, "expert", split_axis=0, concat_axis=0, tiled=True),
        lax.all_to_all(sent_d, "expert", split_axis=0, concat_axis=0, tiled=True),
    )
    partial_value, grad_gate, grad_up, grad_down = expert_backward(
        rows_x, rows_d, w_gate, w_up, w_down
    )
    summed = lax.psum(partial_value.astype(jnp.bfloat16), "tensor").astype(jnp.float32)
    returned = lax.dynamic_slice_in_dim(
        summed, lax.axis_index("tensor") * feat_width, feat_width, 3
    ).astype(jnp.bfloat16)
    arrived = lax.all_to_all(returned, "expert", split_axis=0, concat_axis=0, tiled=True).reshape(
        experts * capacity, feat_width
    )
    masked = jnp.where(occupied[:, None], arrived.astype(jnp.float32), jnp.zeros((), jnp.float32))
    grad_tokens = jax.ops.segment_sum(masked, owner, num_segments=tok_count).astype(jnp.bfloat16)
    return (grad_tokens, grad_gate, grad_up, grad_down)


def solution(mesh):
    return jax.shard_map(
        on_device,
        mesh=mesh,
        in_specs=(
            P("expert", "tensor"),
            P("expert", "tensor"),
            P("expert", None),
            P("expert", None),
            P("expert", "tensor", None),
            P("expert", "tensor", None),
            P("expert", "tensor", None),
        ),
        out_specs=(
            P("expert", "tensor"),
            P("expert", "tensor", None),
            P("expert", "tensor", None),
            P("expert", "tensor", None),
        ),
        check_vma=False,
    )
```

profile of v0, /device:TPU:15, one launch (start us, length us, event | category | flops | bytes accessed | tf_op | source)
XLA Modules:
  0.0 448.9 jit_solution(7881900945583448381)
XLA Ops:
  7.2 0.0 copy-start
  7.2 0.8 copy.49
  8.0 0.1 eq.43
  8.1 0.1 eq.39
  8.2 0.9 reduce-window.6
  9.1 0.2 slice_reduce_fusion
  9.4 0.1 fusion.47
  9.5 0.1 reduce_sum.34
  9.6 0.1 copy.52
  9.7 0.7 multiply_add_fusion
  10.4 0.1 copy.53
  10.5 0.3 fusion.33
  10.9 0.1 broadcast_in_dim.73
  11.0 13.7 %all_gather.7 = bf16[48,4096]{1,0:T(8,128)(2,1)S(1)} all-gather(bf16[48,512]{1,0:T(8,128)(2,1)} %param.7), channel_id=1, replica_groups=mesh['expert'=64,'tensor'=8] {'tensor'}, dimensions={1}, use_global_device_ids=true | all-gather | bytes 442368 | tf_op jit(solution)/shard_map/all_gather | solution.py:59
  24.6 4.3 gather_fusion.1
  29.0 4.5 %bitcast_select_fusion = bf16[64,1,8,4096]{3,2,1,0:T(8,128)(2,1)} fusion(bf16[512,4096]{1,0:T(8,128)(2,1)} %gather_fusion.1, pred[64,8]{1,0:T(8,128)(4,1)S(1)} %broadcast_in_dim.73), kind=kLoop, calls=%fused_computation.16 | loop fusion | flops 2097152 | bytes 8389120 | tf_op jit(solution)/shard_map/jit(_where)/select_n | solution.py:62
  33.5 0.0 copy-start.3
  33.5 0.0 copy-start.2
  33.5 16.3 %all-to-all-start.1 = ((bf16[64,1,8,4096]{3,2,1,0:T(8,128)(2,1)}), bf16[64,1,8,4096]{3,2,1,0:T(8,128)(2,1)}, u32[]{:S(2)}, u32[]{:S(2)}) async-start(bf16[64,1,8,4096]{3,2,1,0:T(8,128)(2,1)} %bitcast_select_fusion), calls=%async_computation.1 | async-start | bytes 8388608 | tf_op jit(solution)/shard_map/all_to_all | solution.py:67
  49.8 0.0 copy-done.3
  49.9 0.1 copy.54
  49.9 0.2 select_reduce_fusion
  50.1 0.1 mul.57
  50.2 0.0 copy-done.2
  50.2 13.5 %all_gather.6 = bf16[48,4096]{1,0:T(8,128)(2,1)S(1)} all-gather(bf16[48,512]{1,0:T(8,128)(2,1)S(1)} %copy-done.2), channel_id=1, replica_groups=mesh['expert'=64,'tensor'=8] {'tensor'}, dimensions={1}, use_global_device_ids=true | all-gather | bytes 442368 | tf_op jit(solution)/shard_map/all_gather | solution.py:60
  63.8 4.4 gather_fusion
  68.1 5.6 %fusion = bf16[64,1,8,4096]{3,2,1,0:T(8,128)(2,1)} fusion(bf16[512,4096]{1,0:T(8,128)(2,1)} %gather_fusion, f32[64,8]{1,0:T(8,128)S(1)} %mul.57), kind=kLoop, calls=%fused_computation.4 | loop fusion | flops 6291456 | bytes 8390656 | tf_op jit(solution)/shard_map/convert_element_type | solution.py:63
  73.8 84.2 %all-to-all-done.1 = bf16[64,1,8,4096]{3,2,1,0:T(8,128)(2,1)} async-done(((bf16[64,1,8,4096]{3,2,1,0:T(8,128)(2,1)}), bf16[64,1,8,4096]{3,2,1,0:T(8,128)(2,1)}, u32[]{:S(2)}, u32[]{:S(2)}) %all-to-all-start.1) | async-done | bytes 4194336 | tf_op jit(solution)/shard_map/all_to_all | solution.py:67
  158.0 33.7 %all-to-all-start = ((bf16[64,1,8,4096]{3,2,1,0:T(8,128)(2,1)}), bf16[64,1,8,4096]{3,2,1,0:T(8,128)(2,1)}, u32[]{:S(2)}, u32[]{:S(2)}) async-start(bf16[64,1,8,4096]{3,2,1,0:T(8,128)(2,1)} %fusion), calls=%async_computation | async-start | bytes 8388608 | tf_op jit(solution)/shard_map/all_to_all | solution.py:68
  191.7 0.0 copy-start.1
  191.7 0.0 copy-start.4
  191.7 0.2 all-reduce.2.cloned.1.call-start
  191.9 0.0 copy-done
  191.9 3.6 fusion.23
  195.5 0.0 copy-done.1
  195.5 3.4 fusion.20
  198.9 105.7 %all-to-all-done = bf16[64,1,8,4096]{3,2,1,0:T(8,128)(2,1)} async-done(((bf16[64,1,8,4096]{3,2,1,0:T(8,128)(2,1)}), bf16[64,1,8,4096]{3,2,1,0:T(8,128)(2,1)}, u32[]{:S(2)}, u32[]{:S(2)}) %all-to-all-start) | async-done | bytes 4194336 | tf_op jit(solution)/shard_map/all_to_all | solution.py:68
  304.6 0.0 copy-done.4
  304.6 3.4 fusion.40
  308.1 1.2 fusion.27
  309.3 3.2 fusion.1
  312.6 0.0 all-reduce.2.cloned.1.call-update
  312.6 91.5 %all-reduce.2.cloned.1.call-done = bf16[64,1,8,4096]{3,2,0,1:T(8,128)(2,1)} async-done(((bf16[64,1,8,4096]{3,2,0,1:T(8,128)(2,1)}), bf16[64,1,8,4096]{3,2,0,1:T(8,128)(2,1)}) %all-reduce.2.cloned.1.call-update) | async-done | bytes 4194320 | tf_op jit(solution)/shard_map/psum | solution.py:73
  404.0 1.9 fusion.35
  405.9 12.8 %all-to-all-start.2 = ((bf16[64,1,8,512]{3,2,1,0:T(8,128)(2,1)}), bf16[64,1,8,512]{3,2,1,0:T(8,128)(2,1)S(1)}, u32[]{:S(2)}, u32[]{:S(2)}) async-start(bf16[64,1,8,512]{3,2,1,0:T(8,128)(2,1)} %fusion.35), calls=%async_computation.2 | async-start | bytes 1048576 | tf_op jit(solution)/shard_map/all_to_all | solution.py:77
  418.8 3.9 fusion.6
  422.7 3.9 fusion.7
  426.6 3.9 fusion.5
  430.6 7.1 %all-to-all-done.2 = bf16[64,1,8,512]{3,2,1,0:T(8,128)(2,1)S(1)} async-done(((bf16[64,1,8,512]{3,2,1,0:T(8,128)(2,1)}), bf16[64,1,8,512]{3,2,1,0:T(8,128)(2,1)S(1)}, u32[]{:S(2)}, u32[]{:S(2)}) %all-to-all-start.2) | async-done | bytes 524320 | tf_op jit(solution)/shard_map/all_to_all | solution.py:77
  437.7 3.8 scatter_custom_fusion
  441.4 0.6 convert_element_type.99
  (5 shorter events, 0.1 us)
Async XLA Ops:
  7.2 184.7 %copy-start = (bf16[1,96,4096]{2,1,0:T(8,128)(2,1)S(1)}, bf16[1,96,4096]{2,1,0:T(8,128)(2,1)}, u32[]{:S(2)}) copy-start(bf16[1,96,4096]{2,1,0:T(8,128)(2,1)} %param.11) | copy-start | bytes 2359300
  33.5 16.4 %copy-start.3 = (f32[48,8]{0,1:T(8,128)S(1)}, f32[48,8]{0,1:T(8,128)}, u32[]{:S(2)}) copy-start(f32[48,8]{0,1:T(8,128)} %param.10) | copy-start | bytes 4612
  33.5 16.7 %copy-start.2 = (bf16[48,512]{1,0:T(8,128)(2,1)S(1)}, bf16[48,512]{1,0:T(8,128)(2,1)}, u32[]{:S(2)}) copy-start(bf16[48,512]{1,0:T(8,128)(2,1)} %param.8) | copy-start | bytes 147460
  33.5 124.5 %all-to-all-start.1 = ((bf16[64,1,8,4096]{3,2,1,0:T(8,128)(2,1)}), bf16[64,1,8,4096]{3,2,1,0:T(8,128)(2,1)}, u32[]{:S(2)}, u32[]{:S(2)}) async-start(bf16[64,1,8,4096]{3,2,1,0:T(8,128)(2,1)} %bitcast_select_fusion), calls=%async_computation.1 | async-start | bytes 8388608 | tf_op jit(solution)/shard_map/all_to_all | solution.py:67
  158.0 146.7 %all-to-all-start = ((bf16[64,1,8,4096]{3,2,1,0:T(8,128)(2,1)}), bf16[64,1,8,4096]{3,2,1,0:T(8,128)(2,1)}, u32[]{:S(2)}, u32[]{:S(2)}) async-start(bf16[64,1,8,4096]{3,2,1,0:T(8,128)(2,1)} %fusion), calls=%async_computation | async-start | bytes 8388608 | tf_op jit(solution)/shard_map/all_to_all | solution.py:68
  191.7 3.8 copy-start.1
  191.7 113.0 %copy-start.4 = (bf16[1,96,4096]{2,1,0:T(8,128)(2,1)S(1)}, bf16[1,96,4096]{2,1,0:T(8,128)(2,1)}, u32[]{:S(2)}) copy-start(bf16[1,96,4096]{2,1,0:T(8,128)(2,1)} %param.13) | copy-start | bytes 2359300
  191.7 212.4 %all-reduce.2.cloned.1.call-start = ((), (), s32[]{:S(2)}) async-start(), calls=%async_computation.3 | async-start | bytes 8388608 | tf_op jit(solution)/shard_map/psum | solution.py:73
  405.9 31.7 %all-to-all-start.2 = ((bf16[64,1,8,512]{3,2,1,0:T(8,128)(2,1)}), bf16[64,1,8,512]{3,2,1,0:T(8,128)(2,1)S(1)}, u32[]{:S(2)}, u32[]{:S(2)}) async-start(bf16[64,1,8,512]{3,2,1,0:T(8,128)(2,1)} %fusion.35), calls=%async_computation.2 | async-start | bytes 1048576 | tf_op jit(solution)/shard_map/all_to_all | solution.py:77
Sparse Core Ops, SparseCore 0:
  312.7 91.2 all-reduce.1
where the time goes:
time: 450 us; the launch traced here: 449 us
  waiting for transfers between devices  288 us (64%)
  starting transfers between devices  63.1 us (14%)
  blocking collectives  27.2 us (6%)
  matrix products  26.7 us (6%)
  other arithmetic  18.7 us (4%)
  between operations  14.2 us (3%)
  local copies, waits for them, and re-layouts  10.5 us (2%)
    all_to_all x1, waiting for transfers between devices, on_device(): lax.all_to_all(sent_d, 'expert', split_axis=0, concat_axis=0, tiled=True)  106 us
    psum x1, waiting for transfers between devices, on_device(): lax.psum(partial_value.astype(jnp.bfloat16), 'tensor').astype(jnp.float32)  91.5 us
    all_to_all x1, waiting for transfers between devices, on_device(): lax.all_to_all(sent_x, 'expert', split_axis=0, concat_axis=0, tiled=True)  84.2 us
    all_to_all x1, starting transfers between devices, on_device(): lax.all_to_all(sent_d, 'expert', split_axis=0, concat_axis=0, tiled=True)  33.7 us
    all_to_all x1, starting transfers between devices, on_device(): lax.all_to_all(sent_x, 'expert', split_axis=0, concat_axis=0, tiled=True)  16.3 us
    all_gather x1, blocking collectives, on_device(): lax.all_gather(tokens, 'tensor', axis=1, tiled=True)  13.7 us
    all_gather x1, blocking collectives, on_device(): lax.all_gather(cotangent, 'tensor', axis=1, tiled=True)  13.5 us
    all_to_all x1, starting transfers between devices, on_device(): lax.all_to_all(returned, 'expert', split_axis=0, concat_axis=0, tiled=True)  12.8 us
  transfers between devices with their start and end apart: 4, of which 4 were waited for; matrix products, arithmetic and copies ran while one was open for 6% of the time, Pallas kernels for 0%

commit v1 on v0

--- a/solution.py
+++ b/solution.py
@@ -4,6 +4,28 @@
 from jax.sharding import PartitionSpec as P
 
 TOP = 8
+
+
+def laid_out(blocks, dim):
+    blocks = jnp.moveaxis(blocks, 0, dim)
+    lengths = blocks.shape
+    return blocks.reshape(*lengths[:dim], lengths[dim] * lengths[dim + 1], *lengths[dim + 2 :])
+
+
+def ring_gather(x, axis, dim):
+    count = lax.axis_size(axis)
+    pairs = [(i, (i + 1) % count) for i in range(count)]
+    back = [(b, a) for a, b in pairs]
+    lower, upper = ([], [])
+    for turn in range(count - 1):
+        if turn % 2 == 0:
+            lower.append(lax.ppermute(lower[-1] if lower else x, axis, pairs))
+        else:
+            upper.append(lax.ppermute(upper[-1] if upper else x, axis, back))
+    blocks = jnp.stack([*lower[::-1], x, *upper])
+    shift = lax.axis_index(axis) - len(lower)
+    blocks = blocks[(jnp.arange(count) - shift) % count]
+    return laid_out(blocks, dim)
 
 
 def expert_backward(rows_x, rows_d, w_gate, w_up, w_down):
@@ -56,7 +78,7 @@
     owner = jnp.sum(jnp.where(by_token, token_iota[None, :], 0), axis=1)
     slot_weight = jnp.sum(jnp.sum(jnp.where(matches, gate_values[None, :, :], 0.0), axis=2), axis=1)
     full_x, full_d = (
-        lax.all_gather(tokens, "tensor", axis=1, tiled=True),
+        ring_gather(tokens, "tensor", 1),
         lax.all_gather(cotangent, "tensor", axis=1, tiled=True),
     )
     sent_x = jnp.where(occupied[:, None], full_x[owner], jnp.zeros((), jnp.bfloat16))

time: 450 us -> 470 us (1.044)
  waiting for transfers between devices: 288 us -> 324 us
  blocking collectives: 27.2 us -> 11.5 us
    psum x1, waiting for transfers between devices: 91.5 us -> 110 us  [on_device(): lax.psum(partial_value.astype(jnp.bfloat16), 'tensor').astype(jnp.float32)]
    all_gather x1 -> x0, blocking collectives: 13.7 us -> none  [on_device(): lax.all_gather(tokens, 'tensor', axis=1, tiled=True)]
    all_to_all x1, starting transfers between devices: 33.7 us -> 21.1 us  [on_device(): lax.all_to_all(sent_d, 'expert', split_axis=0, concat_axis=0, tiled=True)]
    ppermute x0 -> x7, starting transfers between devices: none -> 10.9 us  [the longest x4 10.8 us: ring_gather(): lower.append(lax.ppermute(lower[-1] if lower else x, axis, pairs))]
    all_to_all x1, waiting for transfers between devices: 106 us -> 114 us  [on_device(): lax.all_to_all(sent_d, 'expert', split_axis=0, concat_axis=0, tiled=True)]
    ppermute x0 -> x7, waiting for transfers between devices: none -> 6.17 us  [the longest x4 3.35 us: ring_gather(): lower.append(lax.ppermute(lower[-1] if lower else x, axis, pairs))]
  transfers between devices with their start and end apart: 4 -> 11, of which waited for: 4 -> 8; matrix products, arithmetic and copies ran while one was open for 6% -> 7% of each run, Pallas kernels for 0% -> 0%
where the time goes in v1:
time: 470 us; the launch traced here: 469 us
  waiting for transfers between devices  324 us (69%)
  starting transfers between devices  61.4 us (13%)
  matrix products  26.7 us (6%)
  other arithmetic  18.7 us (4%)
  between operations  14.3 us (3%)
  local copies, waits for them, and re-layouts  11.9 us (3%)
  blocking collectives  11.5 us (2%)
    all_to_all x1, waiting for transfers between devices, on_device(): lax.all_to_all(sent_d, 'expert', split_axis=0, concat_axis=0, tiled=True)  114 us
    psum x1, waiting for transfers between devices, on_device(): lax.psum(partial_value.astype(jnp.bfloat16), 'tensor').astype(jnp.float32)  110 us
    all_to_all x1, waiting for transfers between devices, on_device(): lax.all_to_all(sent_x, 'expert', split_axis=0, concat_axis=0, tiled=True)  87.2 us
    all_to_all x1, starting transfers between devices, on_device(): lax.all_to_all(sent_d, 'expert', split_axis=0, concat_axis=0, tiled=True)  21.1 us
    all_to_all x1, starting transfers between devices, on_device(): lax.all_to_all(sent_x, 'expert', split_axis=0, concat_axis=0, tiled=True)  16.3 us
    all_to_all x1, starting transfers between devices, on_device(): lax.all_to_all(returned, 'expert', split_axis=0, concat_axis=0, tiled=True)  12.8 us
    all_gather x1, blocking collectives, on_device(): lax.all_gather(cotangent, 'tensor', axis=1, tiled=True)  11.5 us
    ppermute x4, starting transfers between devices, ring_gather(): lower.append(lax.ppermute(lower[-1] if lower else x, axis, pairs))  10.8 us
  transfers between devices with their start and end apart: 11, of which 8 were waited for; matrix products, arithmetic and copies ran while one was open for 7% of the time, Pallas kernels for 0%

profile of v1, /device:TPU:15, one launch (start us, length us, event | category | flops | bytes accessed | tf_op | source)
XLA Modules:
  0.0 468.8 jit_solution(15941746101249131829)
XLA Ops:
  7.2 0.0 copy-start
  7.2 0.8 collective-permute-start
  7.9 0.0 collective-permute-start.4
  8.0 0.8 copy.53
  8.7 0.1 eq.45
  8.8 0.1 eq.41
  8.9 0.9 reduce-window.6
  9.8 0.2 slice_reduce_fusion
  10.1 0.1 fusion.47
  10.2 0.1 reduce_sum.34
  10.3 0.1 copy.56
  10.4 0.7 multiply_add_fusion
  11.1 0.1 copy.57
  11.2 0.3 fusion.33
  11.5 0.0 collective-permute-done
  11.6 3.0 collective-permute-start.1
  14.5 1.2 collective-permute-done.1
  15.7 3.5 collective-permute-start.2
  19.2 0.0 collective-permute-done.4
  19.3 0.0 collective-permute-start.5
  19.3 1.1 collective-permute-done.2
  20.4 3.5 collective-permute-start.3
  24.0 0.1 broadcast_in_dim.74
  24.1 0.0 collective-permute-done.5
  24.1 0.0 collective-permute-start.6
  24.1 1.0 collective-permute-done.3
  25.2 0.8 bitcast_dynamic-update-slice_fusion.3
  26.0 2.8 collective-permute-done.6
  28.8 0.6 gather_fusion.1
  29.4 4.4 gather_fusion.2
  33.8 4.5 bitcast_select_fusion
  38.3 16.3 %all-to-all-start.1 = ((bf16[64,1,8,4096]{3,2,1,0:T(8,128)(2,1)}), bf16[64,1,8,4096]{3,2,1,0:T(8,128)(2,1)}, u32[]{:S(2)}, u32[]{:S(2)}) async-start(bf16[64,1,8,4096]{3,2,1,0:T(8,128)(2,1)} %bitcast_select_fusion), calls=%async_computation.1 | async-start | bytes 8388608 | tf_op jit(solution)/shard_map/all_to_all | solution.py:89
  54.6 0.0 copy-done.3
  54.7 0.1 copy.58
  54.7 0.2 select_reduce_fusion
  54.9 0.1 mul.57
  55.0 0.0 copy-done.2
  55.0 11.5 %all_gather.3 = bf16[48,4096]{1,0:T(8,128)(2,1)S(1)} all-gather(bf16[48,512]{1,0:T(8,128)(2,1)S(1)} %copy-done.2), channel_id=1, replica_groups=mesh['expert'=64,'tensor'=8] {'tensor'}, dimensions={1}, use_global_device_ids=true | all-gather | bytes 442368 | tf_op jit(solution)/shard_map/all_gather | solution.py:82
  66.5 4.4 gather_fusion
  70.9 5.6 %fusion = bf16[64,1,8,4096]{3,2,1,0:T(8,128)(2,1)} fusion(bf16[512,4096]{1,0:T(8,128)(2,1)} %gather_fusion, f32[64,8]{1,0:T(8,128)S(1)} %mul.57), kind=kLoop, calls=%fused_computation.5 | loop fusion | flops 6291456 | bytes 8390656 | tf_op jit(solution)/shard_map/convert_element_type | solution.py:85
  76.5 87.2 %all-to-all-done.1 = bf16[64,1,8,4096]{3,2,1,0:T(8,128)(2,1)} async-done(((bf16[64,1,8,4096]{3,2,1,0:T(8,128)(2,1)}), bf16[64,1,8,4096]{3,2,1,0:T(8,128)(2,1)}, u32[]{:S(2)}, u32[]{:S(2)}) %all-to-all-start.1) | async-done | bytes 4194336 | tf_op jit(solution)/shard_map/all_to_all | solution.py:89
  163.7 21.1 %all-to-all-start = ((bf16[64,1,8,4096]{3,2,1,0:T(8,128)(2,1)}), bf16[64,1,8,4096]{3,2,1,0:T(8,128)(2,1)}, u32[]{:S(2)}, u32[]{:S(2)}) async-start(bf16[64,1,8,4096]{3,2,1,0:T(8,128)(2,1)} %fusion), calls=%async_computation | async-start | bytes 8388608 | tf_op jit(solution)/shard_map/all_to_all | solution.py:90
  184.9 0.0 copy-start.1
  184.9 0.0 copy-start.4
  184.9 0.2 all-reduce.2.cloned.1.call-start
  185.1 0.0 copy-done
  185.1 3.6 fusion.23
  188.7 0.0 copy-done.1
  188.7 3.4 fusion.20
  192.1 113.7 %all-to-all-done = bf16[64,1,8,4096]{3,2,1,0:T(8,128)(2,1)} async-done(((bf16[64,1,8,4096]{3,2,1,0:T(8,128)(2,1)}), bf16[64,1,8,4096]{3,2,1,0:T(8,128)(2,1)}, u32[]{:S(2)}, u32[]{:S(2)}) %all-to-all-start) | async-done | bytes 4194336 | tf_op jit(solution)/shard_map/all_to_all | solution.py:90
  305.8 0.0 copy-done.4
  305.8 3.4 fusion.40
  309.3 1.2 fusion.27
  310.5 3.2 fusion.1
  313.7 0.0 all-reduce.2.cloned.1.call-update
  313.8 110.2 %all-reduce.2.cloned.1.call-done = bf16[64,1,8,4096]{3,2,0,1:T(8,128)(2,1)} async-done(((bf16[64,1,8,4096]{3,2,0,1:T(8,128)(2,1)}), bf16[64,1,8,4096]{3,2,0,1:T(8,128)(2,1)}) %all-reduce.2.cloned.1.call-update) | async-done | bytes 4194320 | tf_op jit(solution)/shard_map/psum | solution.py:95
  423.9 1.9 fusion.35
  425.8 12.8 %all-to-all-start.2 = ((bf16[64,1,8,512]{3,2,1,0:T(8,128)(2,1)}), bf16[64,1,8,512]{3,2,1,0:T(8,128)(2,1)S(1)}, u32[]{:S(2)}, u32[]{:S(2)}) async-start(bf16[64,1,8,512]{3,2,1,0:T(8,128)(2,1)} %fusion.35), calls=%async_computation.2 | async-start | bytes 1048576 | tf_op jit(solution)/shard_map/all_to_all | solution.py:99
  438.7 3.9 fusion.6
  442.6 3.9 fusion.7
  446.5 3.9 fusion.5
  450.5 7.1 %all-to-all-done.2 = bf16[64,1,8,512]{3,2,1,0:T(8,128)(2,1)S(1)} async-done(((bf16[64,1,8,512]{3,2,1,0:T(8,128)(2,1)}), bf16[64,1,8,512]{3,2,1,0:T(8,128)(2,1)S(1)}, u32[]{:S(2)}, u32[]{:S(2)}) %all-to-all-start.2) | async-done | bytes 524320 | tf_op jit(solution)/shard_map/all_to_all | solution.py:99
  457.6 3.8 scatter_custom_fusion
  461.3 0.6 convert_element_type.99
  (17 shorter events, 0.2 us)
Async XLA Ops:
  7.2 178.0 %copy-start = (bf16[1,96,4096]{2,1,0:T(8,128)(2,1)S(1)}, bf16[1,96,4096]{2,1,0:T(8,128)(2,1)}, u32[]{:S(2)}) copy-start(bf16[1,96,4096]{2,1,0:T(8,128)(2,1)} %param.11) | copy-start | bytes 2359300
  7.2 4.4 collective-permute-start
  7.9 11.3 %collective-permute-start.4 = (bf16[48,512]{1,0:T(8,128)(2,1)}, bf16[48,512]{1,0:T(8,128)(2,1)S(1)}, u32[]{:S(2)}, u32[]{:S(2)}) collective-permute-start(bf16[48,512]{1,0:T(8,128)(2,1)} %param.7), channel_id=1, source_target_pairs={{1,0},{2,1},{3,2},{4,3},{5,4},{6,5},{7,6},{0,7},{9,8},{10,9},{11,1... | collective-permute-start | bytes 147464 | tf_op jit(solution)/shard_map/ppermute | solution.py:24
  11.6 4.1 collective-permute-start.1
  15.7 4.7 %collective-permute-start.2 = (bf16[48,512]{1,0:T(8,128)(2,1)S(1)}, bf16[48,512]{1,0:T(8,128)(2,1)S(1)}, u32[]{:S(2)}, u32[]{:S(2)}) collective-permute-start(bf16[48,512]{1,0:T(8,128)(2,1)S(1)} %collective-permute-done.1), channel_id=1, source_target_pairs={{0,1},{1,2},{2,3},{3,4},{4,5},{5,6},{6,7},{7,0},{8,9},{9,10},{10,1... | collective-permute-start | bytes 147464 | tf_op jit(solution)/shard_map/ppermute | solution.py:22
  19.3 4.8 %collective-permute-start.5 = (bf16[48,512]{1,0:T(8,128)(2,1)S(1)}, bf16[48,512]{1,0:T(8,128)(2,1)S(1)}, u32[]{:S(2)}, u32[]{:S(2)}) collective-permute-start(bf16[48,512]{1,0:T(8,128)(2,1)S(1)} %collective-permute-done.4), channel_id=1, source_target_pairs={{1,0},{2,1},{3,2},{4,3},{5,4},{6,5},{7,6},{0,7},{9,8},{10,9},{11,1... | collective-permute-start | bytes 147464 | tf_op jit(solution)/shard_map/ppermute | solution.py:24
  20.4 4.7 %collective-permute-start.3 = (bf16[48,512]{1,0:T(8,128)(2,1)S(1)}, bf16[48,512]{1,0:T(8,128)(2,1)S(1)}, u32[]{:S(2)}, u32[]{:S(2)}) collective-permute-start(bf16[48,512]{1,0:T(8,128)(2,1)S(1)} %collective-permute-done.2), channel_id=1, source_target_pairs={{0,1},{1,2},{2,3},{3,4},{4,5},{5,6},{6,7},{7,0},{8,9},{9,10},{10,1... | collective-permute-start | bytes 147464 | tf_op jit(solution)/shard_map/ppermute | solution.py:22
  24.1 4.7 %collective-permute-start.6 = (bf16[48,512]{1,0:T(8,128)(2,1)S(1)}, bf16[48,512]{1,0:T(8,128)(2,1)S(1)}, u32[]{:S(2)}, u32[]{:S(2)}) collective-permute-start(bf16[48,512]{1,0:T(8,128)(2,1)S(1)} %collective-permute-done.5), channel_id=1, source_target_pairs={{1,0},{2,1},{3,2},{4,3},{5,4},{6,5},{7,6},{0,7},{9,8},{10,9},{11,1... | collective-permute-start | bytes 147464 | tf_op jit(solution)/shard_map/ppermute | solution.py:24
  38.3 16.4 %copy-start.3 = (f32[48,8]{0,1:T(8,128)S(1)}, f32[48,8]{0,1:T(8,128)}, u32[]{:S(2)}) copy-start(f32[48,8]{0,1:T(8,128)} %param.10) | copy-start | bytes 4612
  38.3 16.7 %copy-start.2 = (bf16[48,512]{1,0:T(8,128)(2,1)S(1)}, bf16[48,512]{1,0:T(8,128)(2,1)}, u32[]{:S(2)}) copy-start(bf16[48,512]{1,0:T(8,128)(2,1)} %param.8) | copy-start | bytes 147460
  38.3 125.4 %all-to-all-start.1 = ((bf16[64,1,8,4096]{3,2,1,0:T(8,128)(2,1)}), bf16[64,1,8,4096]{3,2,1,0:T(8,128)(2,1)}, u32[]{:S(2)}, u32[]{:S(2)}) async-start(bf16[64,1,8,4096]{3,2,1,0:T(8,128)(2,1)} %bitcast_select_fusion), calls=%async_computation.1 | async-start | bytes 8388608 | tf_op jit(solution)/shard_map/all_to_all | solution.py:89
  163.7 142.1 %all-to-all-start = ((bf16[64,1,8,4096]{3,2,1,0:T(8,128)(2,1)}), bf16[64,1,8,4096]{3,2,1,0:T(8,128)(2,1)}, u32[]{:S(2)}, u32[]{:S(2)}) async-start(bf16[64,1,8,4096]{3,2,1,0:T(8,128)(2,1)} %fusion), calls=%async_computation | async-start | bytes 8388608 | tf_op jit(solution)/shard_map/all_to_all | solution.py:90
  184.9 3.8 copy-start.1
  184.9 120.9 %copy-start.4 = (bf16[1,96,4096]{2,1,0:T(8,128)(2,1)S(1)}, bf16[1,96,4096]{2,1,0:T(8,128)(2,1)}, u32[]{:S(2)}) copy-start(bf16[1,96,4096]{2,1,0:T(8,128)(2,1)} %param.13) | copy-start | bytes 2359300
  184.9 239.1 %all-reduce.2.cloned.1.call-start = ((), (), s32[]{:S(2)}) async-start(), calls=%async_computation.3 | async-start | bytes 8388608 | tf_op jit(solution)/shard_map/psum | solution.py:95
  425.8 31.7 %all-to-all-start.2 = ((bf16[64,1,8,512]{3,2,1,0:T(8,128)(2,1)}), bf16[64,1,8,512]{3,2,1,0:T(8,128)(2,1)S(1)}, u32[]{:S(2)}, u32[]{:S(2)}) async-start(bf16[64,1,8,512]{3,2,1,0:T(8,128)(2,1)} %fusion.35), calls=%async_computation.2 | async-start | bytes 1048576 | tf_op jit(solution)/shard_map/all_to_all | solution.py:99
Sparse Core Ops, SparseCore 0:
  313.9 110.0 all-reduce.1
